TPU v7x, 32 devices: a whole 2x2x4 slice. The times are simulated.
32 devices in a mesh: groups: 2 (over y), latent: 4 (over z), rows: 4 (over x, core).
Axes of the slice: x: 2, y: 2, z: 4, core: 2. Of those that a mesh axis runs over, the one named last changes fastest.
Arguments:
- activations_in: bfloat16 [2, 128, 2304], P('groups', None, 'latent'), parts along dimension 0, may hold values from -6 to 6
- gate_proj: bfloat16 [2304, 4608], P('rows', 'latent'), may hold values from -0.125 to 0.125
- up_proj: bfloat16 [2304, 4608], P('rows', 'latent'), may hold values from -0.125 to 0.125
- down_proj: bfloat16 [4608, 2304], P('latent', 'rows'), may hold values from -0.09375 to 0.09375
- enc_weight: bfloat16 [4608, 65536], P(('groups', 'rows'), 'latent'), parts along dimension 0, may hold values from -6 to 6
- enc_bias: float32 [131072], P(('groups', 'latent')), parts along dimension 0, may hold values from -0.5 to 0.5
- dec_weight: bfloat16 [131072, 2304], P(('groups', 'latent'), 'rows'), parts along dimension 0, may hold values from -6 to 6
- dec_bias: float32 [4608], P(('groups', 'rows')), parts along dimension 0, may hold values from -0.5 to 0.5
Outputs:
- enc_weight_new: bfloat16 [4608, 65536], P(('groups', 'rows'), 'latent'), parts along dimension 0
- enc_bias_new: float32 [131072], P(('groups', 'latent')), parts along dimension 0
- dec_weight_new: bfloat16 [131072, 2304], P(('groups', 'latent'), 'rows'), parts along dimension 0
- dec_bias_new: float32 [4608], P(('groups', 'rows')), parts along dimension 0
There are 2 independent parts, one for each index of `groups`. A program takes and returns all parts, laid end to end along the dimension named above; an argument that names none is the same for every part. Nothing has to cross between parts.
All inputs are finite; a program needn't handle non-finite values.
Results may differ from a plain program's by a relative error of at most 0.02.
Values may be sent and summed in bfloat16 or wider, within the bound.
A program may use at most 128 MiB of HBM per device.

v0:
```python
import jax
import jax.numpy as jnp
from jax import lax
from jax.sharding import PartitionSpec as P

MODEL_WIDTH = 2304
LATENTS = 65536
sparsity_cost = 0.1
sharpness = 8.0
weight_rate = 2.0
enc_bias_rate = 0.01
dec_bias_rate = 0.002


def row_total(term):
    return lax.psum(term.astype(jnp.bfloat16), "rows").astype(jnp.float32)


def body(activations_in, gate_proj, up_proj, down_proj, enc_weight, enc_bias, dec_weight, dec_bias):
    gate_full, up_full = (
        lax.all_gather(gate_proj, "rows", axis=0, tiled=True),
        lax.all_gather(up_proj, "rows", axis=0, tiled=True),
    )
    batches = activations_in.shape[0]
    batch_tokens = activations_in.shape[1]
    all_tokens = batches * batch_tokens
    token_rows = activations_in.reshape(all_tokens, activations_in.shape[2])
    portion = lax.all_gather(token_rows, "latent", axis=1, tiled=True)
    gate_term = jnp.dot(portion, gate_full, preferred_element_type=jnp.float32)
    up_term = jnp.dot(portion, up_full, preferred_element_type=jnp.float32)
    hidden = (jax.nn.gelu(gate_term, approximate=True) * up_term).astype(jnp.bfloat16)
    partial_value = jnp.dot(hidden, down_proj, preferred_element_type=jnp.float32)
    features = lax.psum(partial_value, "latent").astype(jnp.bfloat16)
    features = features.reshape(batches, batch_tokens, features.shape[1])
    enc_scale = MODEL_WIDTH ** (-0.5)
    dec_scale = LATENTS ** (-0.5)
    inputs = features[0]
    local_pre = jnp.dot(inputs, enc_weight, preferred_element_type=jnp.float32)
    pre_latent = enc_scale * row_total(local_pre) + enc_bias
    latents = (jax.nn.softplus(sharpness * pre_latent) / sharpness).astype(jnp.bfloat16)
    local_rebuilt = jnp.dot(latents, dec_weight, preferred_element_type=jnp.float32)
    rebuilt_share = lax.psum_scatter(local_rebuilt, "latent", scatter_dimension=1, tiled=True)
    share_cols = rebuilt_share.shape[1]
    col_offset = lax.axis_index("latent") * share_cols
    inputs_here = lax.dynamic_slice_in_dim(inputs, col_offset, share_cols, 1)
    bias_here = lax.dynamic_slice_in_dim(dec_bias, col_offset, share_cols, 0)
    grad_share = (
        2.0 * (dec_scale * rebuilt_share + bias_here - inputs_here.astype(jnp.float32))
    ).astype(jnp.bfloat16)
    residual_grad = lax.all_gather(grad_share, "latent", axis=1, tiled=True)
    local_back = lax.dot_general(
        residual_grad, dec_weight, (((1,), (1,)), ((), ())), preferred_element_type=jnp.float32
    )
    back_sum = row_total(local_back)
    latent_grad = (
        jax.nn.sigmoid(sharpness * pre_latent) * (dec_scale * back_sum + sparsity_cost)
    ).astype(jnp.bfloat16)
    dec_grad = dec_scale * lax.dot_general(
        latents, residual_grad, (((0,), (0,)), ((), ())), preferred_element_type=jnp.float32
    )
    enc_grad = enc_scale * lax.dot_general(
        inputs, latent_grad, (((0,), (0,)), ((), ())), preferred_element_type=jnp.float32
    )
    enc_bias = enc_bias - enc_bias_rate * jnp.sum(latent_grad, axis=0, dtype=jnp.float32)
    dec_bias = dec_bias - dec_bias_rate * jnp.sum(residual_grad, axis=0, dtype=jnp.float32)
    enc_weight = (enc_weight.astype(jnp.float32) - weight_rate * enc_grad).astype(jnp.bfloat16)
    dec_weight = (dec_weight.astype(jnp.float32) - weight_rate * dec_grad).astype(jnp.bfloat16)
    return (enc_weight, enc_bias, dec_weight, dec_bias)


def solution(mesh):
    return jax.shard_map(
        body,
        mesh=mesh,
        in_specs=(
            P("groups", None, "latent"),
            P("rows", "latent"),
            P("rows", "latent"),
            P("latent", "rows"),
            P(("groups", "rows"), "latent"),
            P(("groups", "latent")),
            P(("groups", "latent"), "rows"),
            P(("groups", "rows")),
        ),
        out_specs=(
            P(("groups", "rows"), "latent"),
            P(("groups", "latent")),
            P(("groups", "latent"), "rows"),
            P(("groups", "rows")),
        ),
        check_vma=False,
    )
```

profile of v0, /device:TPU:0, one launch (start us, length us, event | category | flops | bytes accessed | tf_op | source)
XLA Modules:
  0.0 395.9 jit_solution(4908214912626969955)
XLA Ops:
  7.2 0.7 all-gather.4.cloned.1.call-update
  8.0 0.7 all-gather.6.cloned.1.call-update
  8.7 18.5 %all-gather = bf16[1,128,2304]{1,2,0:T(8,128)(2,1)S(1)} all-gather(bf16[1,128,576]{1,2,0:T(8,128)(2,1)} %param.8), channel_id=2, replica_groups=mesh['groups'=2,'latent'=4,'rows'=4] {'latent'}, dimensions={2}, use_global_device_ids=true | all-gather | bytes 737280 | tf_op jit(solution)/shard_map/all_gather | solution.py:28
  27.2 25.9 %all-gather.4.cloned.1.call-done = bf16[2304,1152]{1,0:T(8,128)(2,1)} async-done(((bf16[576,1152]{1,0:T(8,128)(2,1)}), bf16[2304,1152]{1,0:T(8,128)(2,1)}) %all-gather.4.cloned.1.call-update) | async-done | bytes 5308432 | tf_op jit(solution)/shard_map/all_gather | solution.py:21
  53.1 3.5 fusion.14
  56.6 38.9 %all-gather.6.cloned.1.call-done = bf16[2304,1152]{1,0:T(8,128)(2,1)} async-done(((bf16[576,1152]{1,0:T(8,128)(2,1)}), bf16[2304,1152]{1,0:T(8,128)(2,1)}) %all-gather.6.cloned.1.call-update) | async-done | bytes 5308432 | tf_op jit(solution)/shard_map/all_gather | solution.py:22
  95.5 4.0 fusion.3
  99.4 25.3 %all-reduce.7 = bf16[128,576]{0,1:T(8,128)(2,1)S(1)} all-reduce(f32[128,576]{0,1:T(8,128)S(1)} %fusion.3), channel_id=1, replica_groups=mesh['groups'=2,'latent'=4,'rows'=4] {'latent'}, use_global_device_ids=true, to_apply=%region_0.0 | all-reduce | flops 73728 | bytes 442368 | tf_op jit(solution)/shard_map/psum | solution.py:33
  124.8 12.0 %convolution_convert_fusion.1 = bf16[128,16384]{1,0:T(8,128)(2,1)} fusion(bf16[128,576]{0,1:T(8,128)(2,1)S(1)} %all-reduce.7, bf16[576,16384]{1,0:T(8,128)(2,1)} %param.12), kind=kOutput, calls=%fused_computation.4 | convolution fusion | flops 2418016256 | bytes 23216128 | tf_op jit(solution)/shard_map/dot_general | solution.py:38
  136.8 0.2 reduce-scatter.2.cloned.1.call-start
  137.0 82.7 %all-reduce.4.cloned.1.call-done = bf16[128,16384]{1,0:T(8,128)(2,1)} async-done(((bf16[128,16384]{1,0:T(8,128)(2,1)}), bf16[128,16384]{1,0:T(8,128)(2,1)}) %all-reduce.4.cloned.1.call-update) | async-done | bytes 4194320 | tf_op jit(solution)/shard_map/psum | solution.py:16
  219.7 15.9 %fusion.25 = f32[128,576]{0,1:T(8,128)} fusion(bf16[16384,576]{0,1:T(8,128)(2,1)} %param.14, bf16[128,16384]{1,0:T(8,128)(2,1)} %all-reduce.4.cloned.1.call-done, f32[16384]{0:T(1024)S(1)} %copy-done.2), kind=kOutput, calls=%fused_computation.36 | convolution fusion | flops 2441084928 | bytes 23429120 | tf_op jit(solution)/shard_map/dot_general | solution.py:41
  235.7 0.1 dynamic_slice.6
  235.8 20.4 %reduce-scatter.2.cloned.1.call-done = f32[128,144]{0,1:T(8,128)} async-done(((f32[128,576]{0,1:T(8,128)}), f32[128,144]{0,1:T(8,128)}) %reduce-scatter.2.cloned.1.call-update) | async-done | bytes 73744 | tf_op jit(solution)/shard_map/reduce_scatter | solution.py:42
  256.2 1.0 multiply_convert_fusion.1
  257.1 13.5 %all_gather.15 = bf16[128,576]{0,1:T(8,128)(2,1)S(1)} all-gather(bf16[128,144]{0,1:T(8,128)(2,1)S(1)} %multiply_convert_fusion.1), channel_id=1, replica_groups=mesh['groups'=2,'latent'=4,'rows'=4] {'latent'}, dimensions={1}, use_global_device_ids=true | all-gather | bytes 184320 | tf_op jit(solution)/shard_map/all_gather | solution.py:50
  270.6 12.0 %convolution_convert_fusion = bf16[128,16384]{1,0:T(8,128)(2,1)} fusion(bf16[128,576]{0,1:T(8,128)(2,1)S(1)} %all_gather.15, bf16[16384,576]{0,1:T(8,128)(2,1)} %param.14), kind=kOutput, calls=%fused_computation.3 | convolution fusion | flops 2418016256 | bytes 23216128 | tf_op jit(solution)/shard_map/dot_general | solution.py:51
  282.6 0.1 convert_reduce_fusion.1
  282.7 0.6 multiply_subtract_fusion.1
  283.3 32.5 %subtract_convert_fusion = bf16[16384,576]{0,1:T(8,128)(2,1)} fusion(bf16[16384,576]{0,1:T(8,128)(2,1)} %param.14, bf16[128,576]{0,1:T(8,128)(2,1)S(1)} %all_gather.15, bf16[128,16384]{1,0:T(8,128)(2,1)} %all-reduce.4.cloned.1.call-done, f32[16384]{0:T(1024)S(1)} %copy-done.2), kind=kOutput, calls=%fused_computation | convolution fusion | flops 2478833664 | bytes 42156032 | tf_op jit(solution)/shard_map/dot_general | solution.py:58
  315.8 50.7 %all-reduce.6.cloned.1.call-done = bf16[128,16384]{1,0:T(8,128)(2,1)} async-done(((bf16[128,16384]{1,0:T(8,128)(2,1)}), bf16[128,16384]{1,0:T(8,128)(2,1)}) %all-reduce.6.cloned.1.call-update) | async-done | bytes 4194320 | tf_op jit(solution)/shard_map/psum | solution.py:16
  366.5 7.7 %convert_reduce_fusion = (f32[16384]{0:T(1024)S(1)}, bf16[128,16384]{1,0:T(8,128)(2,1)}) fusion(bf16[128,16384]{1,0:T(8,128)(2,1)} %all-reduce.6.cloned.1.call-done, f32[16384]{0:T(1024)S(1)} %copy-done.2, bf16[128,16384]{1,0:T(8,128)(2,1)} %all-reduce.4.cloned.1.call-done), kind=kLoop, calls=%fused_computation.7 | loop fusion | flops 29343744 | bytes 12713984 | tf_op jit(solution)/shard_map/reduce_sum | solution.py:64
  374.2 14.5 %subtract_convert_fusion.1 = bf16[576,16384]{1,0:T(8,128)(2,1)} fusion(bf16[576,16384]{1,0:T(8,128)(2,1)} %param.12, bf16[128,576]{0,1:T(8,128)(2,1)S(1)} %all-reduce.7, bf16[128,16384]{1,0:T(8,128)(2,1)} %get-tuple-element.5), kind=kOutput, calls=%fused_computation.1 | convolution fusion | flops 2453667840 | bytes 42090496 | tf_op jit(solution)/shard_map/dot_general | solution.py:61
  388.7 0.6 multiply_subtract_fusion
  (15 shorter events, 0.2 us)
Async XLA Ops:
  7.2 88.3 %copy-start = (bf16[1152,576]{0,1:T(8,128)(2,1)S(1)}, bf16[1152,576]{0,1:T(8,128)(2,1)}, u32[]{:S(2)}) copy-start(bf16[1152,576]{0,1:T(8,128)(2,1)} %param.11) | copy-start | bytes 3981316
  7.2 45.9 %all-gather.4.cloned.1.call-start = ((), (), s32[]{:S(2)}) async-start(), calls=%async_computation.1 | async-start | bytes 6635520 | tf_op jit(solution)/shard_map/all_gather | solution.py:21
  7.9 87.5 %all-gather.6.cloned.1.call-start = ((), (), s32[]{:S(2)}) async-start(), calls=%async_computation.2 | async-start | bytes 6635520 | tf_op jit(solution)/shard_map/all_gather | solution.py:22
  8.7 211.0 %all-reduce.4.cloned.1.call-start = ((), (), s32[]{:S(2)}) async-start(), calls=%async_computation.3 | async-start | bytes 8388608 | tf_op jit(solution)/shard_map/psum | solution.py:16
  124.7 94.9 %copy-start.2 = (f32[16384]{0:T(1024)S(1)}, f32[16384]{0:T(1024)}, u32[]{:S(2)}) copy-start(f32[16384]{0:T(1024)} %param.13) | copy-start | bytes 196612
  136.8 98.9 %copy-start.3 = (f32[576]{0:T(1024)S(1)}, f32[576]{0:T(1024)}, u32[]{:S(2)}) copy-start(f32[576]{0:T(1024)} %param.15) | copy-start | bytes 6916
  136.8 119.4 %reduce-scatter.2.cloned.1.call-start = ((), (), s32[]{:S(2)}) async-start(), calls=%async_computation.4 | async-start | bytes 368640 | tf_op jit(solution)/shard_map/reduce_scatter | solution.py:42
  235.6 130.9 %all-reduce.6.cloned.1.call-start = ((), (), s32[]{:S(2)}) async-start(), calls=%async_computation.5 | async-start | bytes 8388608 | tf_op jit(solution)/shard_map/psum | solution.py:16
  374.2 15.1 %copy-start.1 = (bf16[1152,576]{0,1:T(8,128)(2,1)S(1)}, bf16[1152,576]{0,1:T(8,128)(2,1)}, u32[]{:S(2)}) copy-start(bf16[1152,576]{0,1:T(8,128)(2,1)} %param.11) | copy-start | bytes 3981316
Sparse Core Ops, SparseCore 0:
  9.5 43.4 all-gather.3
  54.6 40.7 all-gather.5
  136.9 82.7 all-reduce.3
  235.8 20.3 reduce-scatter.1
  282.9 83.6 all-reduce.5
where the time goes:
time: 396 us
  waiting for transfers between devices  220 us (56%)
  matrix products  94.3 us (24%)
  blocking collectives  57.3 us (14%)
  between operations  13.8 us (3%)
  other arithmetic  10 us (3%)
    psum x2, waiting for transfers between devices, row_total(): return lax.psum(term.astype(jnp.bfloat16), 'rows').astype(jnp.float32)  133 us
    all_gather x1, waiting for transfers between devices, body(): lax.all_gather(up_proj, 'rows', axis=0, tiled=True)  38.9 us
    dot_general x1, matrix products, body(): lax.dot_general(latents, residual_grad, (((0,), (0,)), ((), ())), preferr...  32.5 us
    all_gather x1, waiting for transfers between devices, body(): lax.all_gather(gate_proj, 'rows', axis=0, tiled=True)  25.9 us
    psum x1, blocking collectives, body(): features = lax.psum(partial_value, 'latent').astype(jnp.bfloat16)  25.3 us
    reduce_scatter x1, waiting for transfers between devices, body(): lax.psum_scatter(local_rebuilt, 'latent', scatter_dimension=1, tiled=True)  20.4 us
    all_gather x1, blocking collectives, body(): portion = lax.all_gather(token_rows, 'latent', axis=1, tiled=True)  18.5 us
    dot_general x1, matrix products, body(): jnp.dot(latents, dec_weight, preferred_element_type=jnp.float32)  15.9 us
  transfers between devices with their start and end apart: 5, of which 5 were waited for; matrix products, arithmetic and copies ran while one was open for 9% of the time, Pallas kernels for 0%

commit v1 on v0

--- a/solution.py
+++ b/solution.py
@@ -12,6 +12,19 @@
 dec_bias_rate = 0.002
 
 
+def collect(x, axis, dim):
+    ways = lax.axis_size(axis)
+    up = [(d, (d + 1) % ways) for d in range(ways)]
+    down = [(d, (d - 1) % ways) for d in range(ways)]
+    earlier, later = ([x], [x])
+    for _ in range(ways // 2):
+        earlier.append(lax.ppermute(earlier[-1], axis, up))
+    for _ in range((ways - 1) // 2):
+        later.append(lax.ppermute(later[-1], axis, down))
+    line = jnp.concatenate([*earlier[::-1], *later[1:]], axis=dim)
+    return jnp.roll(line, (lax.axis_index(axis) - ways // 2) * x.shape[dim], axis=dim)
+
+
 def row_total(term):
     return lax.psum(term.astype(jnp.bfloat16), "rows").astype(jnp.float32)
 
@@ -19,7 +32,7 @@
 def body(activations_in, gate_proj, up_proj, down_proj, enc_weight, enc_bias, dec_weight, dec_bias):
     gate_full, up_full = (
         lax.all_gather(gate_proj, "rows", axis=0, tiled=True),
-        lax.all_gather(up_proj, "rows", axis=0, tiled=True),
+        collect(up_proj, "rows", 0),
     )
     batches = activations_in.shape[0]
     batch_tokens = activations_in.shape[1]

time: 396 us -> 407 us (1.028)
  local copies, waits for them, and re-layouts: 0.11 us -> 18.7 us
  waiting for transfers between devices: 220 us -> 205 us
  starting transfers between devices: 0.38 us -> 4.82 us
    ppermute x0 -> x3, waiting for transfers between devices: none -> 50.4 us  [the longest x2 50.4 us: collect(): earlier.append(lax.ppermute(earlier[-1], axis, up))]
    all_gather x1 -> x0, waiting for transfers between devices: 38.9 us -> none  [body(): lax.all_gather(up_proj, 'rows', axis=0, tiled=True)]
    all_gather x1, waiting for transfers between devices: 25.9 us -> 0.01 us  [body(): lax.all_gather(gate_proj, 'rows', axis=0, tiled=True)]
    unnamed x8 -> x17, local copies, waits for them, and re-layouts: 0.03 us -> 16.1 us
    ppermute x0 -> x3, starting transfers between devices: none -> 4.48 us  [the longest x2 4.48 us: collect(): earlier.append(lax.ppermute(earlier[-1], axis, up))]
  transfers between devices with their start and end apart: 5 -> 7, of which waited for: 5 -> 5; matrix products, arithmetic and copies ran while one was open for 9% -> 13% of each run, Pallas kernels for 0% -> 0%
where the time goes in v1:
time: 407 us; the launch traced here: 406 us
  waiting for transfers between devices  205 us (50%)
  matrix products  95 us (23%)
  blocking collectives  59.1 us (15%)
  local copies, waits for them, and re-layouts  18.7 us (5%)
  between operations  13.9 us (3%)
  other arithmetic  9.97 us (2%)
  starting transfers between devices  4.82 us (1%)
    psum x2, waiting for transfers between devices, row_total(): return lax.psum(term.astype(jnp.bfloat16), 'rows').astype(jnp.float32)  133 us
    ppermute x2, waiting for transfers between devices, collect(): earlier.append(lax.ppermute(earlier[-1], axis, up))  50.4 us
    dot_general x1, matrix products, body(): lax.dot_general(latents, residual_grad, (((0,), (0,)), ((), ())), preferr...  32.5 us
    psum x1, blocking collectives, body(): features = lax.psum(partial_value, 'latent').astype(jnp.bfloat16)  27.5 us
    reduce_scatter x1, waiting for transfers between devices, body(): lax.psum_scatter(local_rebuilt, 'latent', scatter_dimension=1, tiled=True)  20.4 us
    all_gather x1, blocking collectives, body(): portion = lax.all_gather(token_rows, 'latent', axis=1, tiled=True)  18.1 us
    unnamed x17, local copies, waits for them, and re-layouts  16.1 us
    dot_general x1, matrix products, body(): jnp.dot(latents, dec_weight, preferred_element_type=jnp.float32)  15.9 us
  transfers between devices with their start and end apart: 7, of which 5 were waited for; matrix products, arithmetic and copies ran while one was open for 13% of the time, Pallas kernels for 0%

profile of v1, /device:TPU:0, one launch (start us, length us, event | category | flops | bytes accessed | tf_op | source)
XLA Modules:
  0.0 406.4 jit_solution(17516812404903544010)
XLA Ops:
  8.5 23.8 %collective-permute-done = bf16[576,1152]{1,0:T(8,128)(2,1)} collective-permute-done((bf16[576,1152]{1,0:T(8,128)(2,1)}, bf16[576,1152]{1,0:T(8,128)(2,1)}, u32[]{:S(2)}, u32[]{:S(2)}) %collective-permute-start) | collective-permute-done | bytes 1327136 | tf_op jit(solution)/shard_map/ppermute | solution.py:21
  32.3 3.9 collective-permute-start.1
  36.3 18.1 %all-gather = bf16[1,128,2304]{1,2,0:T(8,128)(2,1)S(1)} all-gather(bf16[1,128,576]{1,2,0:T(8,128)(2,1)} %param.8), channel_id=2, replica_groups=mesh['groups'=2,'latent'=4,'rows'=4] {'latent'}, dimensions={2}, use_global_device_ids=true | all-gather | bytes 737280 | tf_op jit(solution)/shard_map/all_gather | solution.py:41
  54.4 26.6 %collective-permute-done.1 = bf16[576,1152]{1,0:T(8,128)(2,1)} collective-permute-done((bf16[576,1152]{1,0:T(8,128)(2,1)}, bf16[576,1152]{1,0:T(8,128)(2,1)}, u32[]{:S(2)}, u32[]{:S(2)}) %collective-permute-start.1) | collective-permute-done | bytes 1327136 | tf_op jit(solution)/shard_map/ppermute | solution.py:21
  80.9 2.5 constant_dynamic-update-slice_fusion.7
  83.4 2.5 constant_dynamic-update-slice_fusion.6
  85.9 2.5 constant_dynamic-update-slice_fusion.5
  88.4 2.5 constant_dynamic-update-slice_fusion.4
  90.9 2.5 constant_dynamic-update-slice_fusion.3
  93.4 2.5 constant_dynamic-update-slice_fusion.2
  97.0 2.5 constant_dynamic-update-slice_fusion
  99.5 3.5 fusion.26
  103.0 4.7 %fusion.14 = f32[128,576]{0,1:T(8,128)S(1)} fusion(bf16[1152,576]{0,1:T(8,128)(2,1)S(1)} %copy-done, bf16[4608,1152]{1,0:T(8,128)(2,1)} %constant_dynamic-update-slice_fusion, s32[]{:T(128)S(6)} %select_n.22, f32[128,1152]{1,0:T(8,128)S(1)} %fusion.26, bf16[1,128,2304]{1,2,0:T(8,128)(2,1)S(1)} %all-gather), kind=kOutput, calls=%fused_computation.15 | convolution fusion | flops 850821120 | bytes 8110084 | tf_op jit(solution)/shard_map/dot_general | solution.py:45
  107.6 27.5 %all-reduce.7 = bf16[128,576]{0,1:T(8,128)(2,1)S(1)} all-reduce(f32[128,576]{0,1:T(8,128)S(1)} %fusion.14), channel_id=1, replica_groups=mesh['groups'=2,'latent'=4,'rows'=4] {'latent'}, use_global_device_ids=true, to_apply=%region_0.1 | all-reduce | flops 73728 | bytes 442368 | tf_op jit(solution)/shard_map/psum | solution.py:46
  135.2 12.0 %convolution_convert_fusion.1 = bf16[128,16384]{1,0:T(8,128)(2,1)} fusion(bf16[128,576]{0,1:T(8,128)(2,1)S(1)} %all-reduce.7, bf16[576,16384]{1,0:T(8,128)(2,1)} %param.12), kind=kOutput, calls=%fused_computation.4 | convolution fusion | flops 2418016256 | bytes 23216128 | tf_op jit(solution)/shard_map/dot_general | solution.py:51
  147.4 82.8 %all-reduce.4.cloned.1.call-done = bf16[128,16384]{1,0:T(8,128)(2,1)} async-done(((bf16[128,16384]{1,0:T(8,128)(2,1)}), bf16[128,16384]{1,0:T(8,128)(2,1)}) %all-reduce.4.cloned.1.call-update) | async-done | bytes 4194320 | tf_op jit(solution)/shard_map/psum | solution.py:29
  230.3 15.9 %fusion.39 = f32[128,576]{0,1:T(8,128)} fusion(bf16[16384,576]{0,1:T(8,128)(2,1)} %param.14, bf16[128,16384]{1,0:T(8,128)(2,1)} %all-reduce.4.cloned.1.call-done, f32[16384]{0:T(1024)S(1)} %copy-done.3), kind=kOutput, calls=%fused_computation.48 | convolution fusion | flops 2441084928 | bytes 23429120 | tf_op jit(solution)/shard_map/dot_general | solution.py:54
  246.3 20.4 %reduce-scatter.2.cloned.1.call-done = f32[128,144]{0,1:T(8,128)} async-done(((f32[128,576]{0,1:T(8,128)}), f32[128,144]{0,1:T(8,128)}) %reduce-scatter.2.cloned.1.call-update) | async-done | bytes 73744 | tf_op jit(solution)/shard_map/reduce_scatter | solution.py:55
  267.7 13.5 %all_gather.11 = bf16[128,576]{0,1:T(8,128)(2,1)S(1)} all-gather(bf16[128,144]{0,1:T(8,128)(2,1)S(1)} %multiply_convert_fusion.1), channel_id=1, replica_groups=mesh['groups'=2,'latent'=4,'rows'=4] {'latent'}, dimensions={1}, use_global_device_ids=true | all-gather | bytes 184320 | tf_op jit(solution)/shard_map/all_gather | solution.py:63
  281.2 12.0 %convolution_convert_fusion = bf16[128,16384]{1,0:T(8,128)(2,1)} fusion(bf16[128,576]{0,1:T(8,128)(2,1)S(1)} %all_gather.11, bf16[16384,576]{0,1:T(8,128)(2,1)} %param.14), kind=kOutput, calls=%fused_computation.3 | convolution fusion | flops 2418016256 | bytes 23216128 | tf_op jit(solution)/shard_map/dot_general | solution.py:64
  293.9 32.5 %subtract_convert_fusion = bf16[16384,576]{0,1:T(8,128)(2,1)} fusion(bf16[16384,576]{0,1:T(8,128)(2,1)} %param.14, bf16[128,576]{0,1:T(8,128)(2,1)S(1)} %all_gather.11, bf16[128,16384]{1,0:T(8,128)(2,1)} %all-reduce.4.cloned.1.call-done, f32[16384]{0:T(1024)S(1)} %copy-done.3), kind=kOutput, calls=%fused_computation | convolution fusion | flops 2478833664 | bytes 42156032 | tf_op jit(solution)/shard_map/dot_general | solution.py:71
  326.4 50.7 %all-reduce.6.cloned.1.call-done = bf16[128,16384]{1,0:T(8,128)(2,1)} async-done(((bf16[128,16384]{1,0:T(8,128)(2,1)}), bf16[128,16384]{1,0:T(8,128)(2,1)}) %all-reduce.6.cloned.1.call-update) | async-done | bytes 4194320 | tf_op jit(solution)/shard_map/psum | solution.py:29
  377.1 7.6 %convert_reduce_fusion = (f32[16384]{0:T(1024)S(1)}, bf16[128,16384]{1,0:T(8,128)(2,1)}) fusion(bf16[128,16384]{1,0:T(8,128)(2,1)} %all-reduce.6.cloned.1.call-done, f32[16384]{0:T(1024)S(1)} %copy-done.3, bf16[128,16384]{1,0:T(8,128)(2,1)} %all-reduce.4.cloned.1.call-done), kind=kLoop, calls=%fused_computation.7 | loop fusion | flops 29343744 | bytes 12713984 | tf_op jit(solution)/shard_map/reduce_sum | solution.py:77
  384.7 14.5 %subtract_convert_fusion.1 = bf16[576,16384]{1,0:T(8,128)(2,1)} fusion(bf16[576,16384]{1,0:T(8,128)(2,1)} %param.12, bf16[128,576]{0,1:T(8,128)(2,1)S(1)} %all-reduce.7, bf16[128,16384]{1,0:T(8,128)(2,1)} %get-tuple-element.5), kind=kOutput, calls=%fused_computation.1 | convolution fusion | flops 2453667840 | bytes 42090496 | tf_op jit(solution)/shard_map/dot_general | solution.py:74
  (28 shorter events, 5.2 us)
Async XLA Ops:
  7.2 95.8 %copy-start = (bf16[1152,576]{0,1:T(8,128)(2,1)S(1)}, bf16[1152,576]{0,1:T(8,128)(2,1)}, u32[]{:S(2)}) copy-start(bf16[1152,576]{0,1:T(8,128)(2,1)} %param.11) | copy-start | bytes 3981316
  7.2 92.3 %all-gather.3.cloned.1.call-start = ((), (), s32[]{:S(2)}) async-start(), calls=%async_computation.1 | async-start | bytes 6635520 | tf_op jit(solution)/shard_map/all_gather | solution.py:34
  7.9 87.9 %copy-start.2 = (bf16[576,1152]{1,0:T(8,128)(2,1)S(1)}, bf16[576,1152]{1,0:T(8,128)(2,1)}, u32[]{:S(2)}) copy-start(bf16[576,1152]{1,0:T(8,128)(2,1)} %param.10) | copy-start | bytes 3981316
  7.9 222.3 %all-reduce.4.cloned.1.call-start = ((), (), s32[]{:S(2)}) async-start(), calls=%async_computation.2 | async-start | bytes 8388608 | tf_op jit(solution)/shard_map/psum | solution.py:29
  8.0 24.4 %collective-permute-start = (bf16[576,1152]{1,0:T(8,128)(2,1)}, bf16[576,1152]{1,0:T(8,128)(2,1)}, u32[]{:S(2)}, u32[]{:S(2)}) collective-permute-start(bf16[576,1152]{1,0:T(8,128)(2,1)} %param.10), channel_id=1, source_target_pairs={{0,1},{1,2},{2,3},{3,0},{4,5},{5,6},{6,7},{7,4},{8,9},{9,10},{10,1... | collective-permute-start | bytes 3981320 | tf_op jit(solution)/shard_map/ppermute | solution.py:21
  32.3 48.6 %collective-permute-start.1 = (bf16[576,1152]{1,0:T(8,128)(2,1)}, bf16[576,1152]{1,0:T(8,128)(2,1)}, u32[]{:S(2)}, u32[]{:S(2)}) collective-permute-start(bf16[576,1152]{1,0:T(8,128)(2,1)} %collective-permute-done), channel_id=1, source_target_pairs={{0,1},{1,2},{2,3},{3,0},{4,5},{5,6},{6,7},{7,4},{8,9},{9,10},{10,1... | collective-permute-start | bytes 3981320 | tf_op jit(solution)/shard_map/ppermute | solution.py:21
  36.3 52.1 %collective-permute-start.2 = (bf16[576,1152]{1,0:T(8,128)(2,1)}, bf16[576,1152]{1,0:T(8,128)(2,1)}, u32[]{:S(2)}, u32[]{:S(2)}) collective-permute-start(bf16[576,1152]{1,0:T(8,128)(2,1)} %param.10), channel_id=1, source_target_pairs={{0,3},{1,0},{2,1},{3,2},{4,7},{5,4},{6,5},{7,6},{8,11},{9,8},{10,9... | collective-permute-start | bytes 3981320 | tf_op jit(solution)/shard_map/ppermute | solution.py:23
  135.2 95.1 %copy-start.3 = (f32[16384]{0:T(1024)S(1)}, f32[16384]{0:T(1024)}, u32[]{:S(2)}) copy-start(f32[16384]{0:T(1024)} %param.13) | copy-start | bytes 196612
  147.2 99.1 %copy-start.4 = (f32[576]{0:T(1024)S(1)}, f32[576]{0:T(1024)}, u32[]{:S(2)}) copy-start(f32[576]{0:T(1024)} %param.15) | copy-start | bytes 6916
  147.2 119.5 %reduce-scatter.2.cloned.1.call-start = ((), (), s32[]{:S(2)}) async-start(), calls=%async_computation.3 | async-start | bytes 368640 | tf_op jit(solution)/shard_map/reduce_scatter | solution.py:55
  246.2 130.9 %all-reduce.6.cloned.1.call-start = ((), (), s32[]{:S(2)}) async-start(), calls=%async_computation.4 | async-start | bytes 8388608 | tf_op jit(solution)/shard_map/psum | solution.py:29
  384.7 15.1 %copy-start.1 = (bf16[1152,576]{0,1:T(8,128)(2,1)S(1)}, bf16[1152,576]{0,1:T(8,128)(2,1)}, u32[]{:S(2)}) copy-start(bf16[1152,576]{0,1:T(8,128)(2,1)} %param.11) | copy-start | bytes 3981316
Sparse Core Ops, SparseCore 0:
  9.5 63.4 all-gather.2
  147.3 82.8 all-reduce.3
  246.3 20.3 reduce-scatter.1
  293.4 83.6 all-reduce.5
